TPU v7x, 32 devices: a whole 2x2x4 slice. The times are simulated.
32 devices in a mesh: src: 2 (over x), tgt: 16 (over z, y, core).
Axes of the slice: x: 2, y: 2, z: 4, core: 2. Of those that a mesh axis runs over, the one named last changes fastest.
Arguments:
- src_emb: bfloat16 [8192, 256], P(('src', 'tgt')), may hold values from -32 to 32
- tgt_emb: bfloat16 [16384, 256], P(('tgt', 'src')), may hold values from -32 to 32
- block_rows: int32 [2, 16, 24], P('src', 'tgt'), may hold values from 0 to 15, as said below
- block_cols: int32 [2, 16, 24], P('src', 'tgt'), may hold values from 0 to 3
- block_counts: int32 [2, 16], P('src', 'tgt'), may hold values from 4 to 24, as said below
Outputs:
- transport: bfloat16 [2, 16, 24, 256, 256], P('src', 'tgt')
- row_potential: float32 [8192], P(('src', 'tgt'))
- col_potential: float32 [16384], P(('tgt', 'src'))
Inputs may be any that keep to these rules, and one draw needn't show every extreme that they name: The 24 slots of one device name distinct blocks (block_rows, block_cols); its first 4 slots name every local block column once; every local block row of a src index is named by a live slot of some device of that index. `block_counts`: exactly 24 on some device.
All inputs are finite; a program needn't handle non-finite values.
Results may differ from a plain program's by a relative error of at most 0.0019.
The roundings to bfloat16 on the way count: a program that leaves them out, or rounds other values in their place, can miss the bound.
Values may be sent and summed in bfloat16 or wider, within the bound.
No kernel may reach another device: no remote copies, remote signals or barrier semaphores. Data moves between devices by JAX's collectives and lax.ppermute only.
A program may use at most 64 MiB of HBM per device.

v0:
```python
import math

import jax
import jax.numpy as jnp
from jax import lax
from jax.sharding import PartitionSpec as P

DIM = 256
BLOCK = 256
ROW_BLOCKS = 16
COL_BLOCKS = 4
SLOTS = 24
ITERS = 3


inv_temp = 250.0
sentinel = -1e30
highest = lax.Precision.HIGHEST


def unit_rows(embedding):
    values = embedding.astype(jnp.float32)
    inverse_norm = lax.rsqrt(jnp.sum(values * values, axis=1, keepdims=True) + 1e-06)
    return (values * inverse_norm).astype(jnp.bfloat16)


def spread_top(slot_top, slot_hot):
    return jnp.max(jnp.where(slot_hot[:, :, None] > 0, slot_top[:, None, :], sentinel), axis=0)


def spread_sum(slot_sums, slot_hot):
    return jnp.einsum("cn,cb->nb", slot_hot, slot_sums, precision=highest)


def row_potential(scores, col_slots, rows_idx, row_hot):
    shifted = scores + col_slots[:, None, :]
    top_local = spread_top(jnp.max(shifted, axis=2), row_hot)
    top_value = lax.pmax(top_local, "tgt")
    slot_sums = jnp.sum(jnp.exp(shifted - top_value[rows_idx][:, :, None]), axis=2)
    sum_total = lax.psum(spread_sum(slot_sums, row_hot), "tgt")
    row_dual = -(top_value + jnp.log(sum_total))
    share_width = row_dual.size // lax.axis_size("tgt")
    own_rows = lax.dynamic_slice_in_dim(
        row_dual.reshape(-1), lax.axis_index("tgt") * share_width, share_width
    )
    return (row_dual, own_rows)


def col_potential(scores, row_slots, cols_idx, col_hot, log_ratio):
    shifted = scores + row_slots[:, :, None]
    top_local = spread_top(jnp.max(shifted, axis=1), col_hot)
    top_value = lax.pmax(top_local, "src")
    slot_sums = jnp.sum(jnp.exp(shifted - top_value[cols_idx][:, None, :]), axis=1)
    sum_total = lax.psum(spread_sum(slot_sums, col_hot), "src")
    return log_ratio - (top_value + jnp.log(sum_total))


def shards(src_emb, tgt_emb, block_rows, block_cols, block_counts):
    src_rows = lax.all_gather(unit_rows(src_emb), "tgt", axis=0, tiled=True)
    tgt_rows = lax.all_gather(unit_rows(tgt_emb), "src", axis=0, tiled=True)
    rows_idx = block_rows[0, 0]
    cols_idx = block_cols[0, 0]
    live_slot = jnp.arange(SLOTS, dtype=jnp.int32) < block_counts[0, 0]
    row_hot = (
        (rows_idx[:, None] == jnp.arange(ROW_BLOCKS, dtype=jnp.int32)[None, :]) & live_slot[:, None]
    ).astype(jnp.float32)
    col_hot = (
        (cols_idx[:, None] == jnp.arange(COL_BLOCKS, dtype=jnp.int32)[None, :]) & live_slot[:, None]
    ).astype(jnp.float32)
    src_blocks = src_rows.reshape(ROW_BLOCKS, BLOCK, DIM)[rows_idx]
    tgt_blocks = tgt_rows.reshape(COL_BLOCKS, BLOCK, DIM)[cols_idx]
    products = jnp.einsum(
        "cbe,cde->cbd", src_blocks, tgt_blocks, preferred_element_type=jnp.float32
    )
    scores = jnp.where(live_slot[:, None, None], products * inv_temp, sentinel)
    log_ratio = math.log(ROW_BLOCKS * lax.axis_size("src") / (COL_BLOCKS * lax.axis_size("tgt")))
    col_dual = jnp.zeros((COL_BLOCKS, BLOCK), jnp.float32)
    row_dual = jnp.zeros((ROW_BLOCKS, BLOCK), jnp.float32)
    own_rows = jnp.zeros((ROW_BLOCKS * BLOCK // lax.axis_size("tgt"),), jnp.float32)
    for sweep in range(ITERS):
        row_dual, own_rows = row_potential(scores, col_dual[cols_idx], rows_idx, row_hot)
        col_dual = col_potential(scores, row_dual[rows_idx], cols_idx, col_hot, log_ratio)
    transport = jnp.exp(
        scores + row_dual[rows_idx][:, :, None] + col_dual[cols_idx][:, None, :]
    ).astype(jnp.bfloat16)
    share_width = col_dual.size // lax.axis_size("src")
    own_cols = lax.dynamic_slice_in_dim(
        col_dual.reshape(-1), lax.axis_index("src") * share_width, share_width
    )
    return (transport[None, None], own_rows / inv_temp, own_cols / inv_temp)


def solution(mesh):
    return jax.shard_map(
        shards,
        mesh=mesh,
        in_specs=(
            P(("src", "tgt"), None),
            P(("tgt", "src"), None),
            P("src", "tgt", None),
            P("src", "tgt", None),
            P("src", "tgt"),
        ),
        out_specs=(P("src", "tgt", None, None, None), P(("src", "tgt")), P(("tgt", "src"))),
        check_vma=False,
    )
```

profile of v0, /device:TPU:0, one launch (start us, length us, event | category | flops | bytes accessed | tf_op | source)
XLA Modules:
  0.0 503.7 jit_solution(15820733972963911582)
XLA Ops:
  8.3 1.7 fusion.4
  11.2 1.1 fusion.1
  12.3 1.1 fusion.2
  13.4 9.9 %all_gather.7 = bf16[1024,256]{1,0:T(8,128)(2,1)S(1)} all-gather(bf16[512,256]{1,0:T(8,128)(2,1)S(1)} %fusion.2), channel_id=1, replica_groups=mesh['src'=2,'tgt'=16] {'src'}, dimensions={0}, use_global_device_ids=true | all-gather | bytes 786432 | tf_op jit(solution)/shard_map/all_gather | solution.py:60
  23.4 2.5 gather_fusion.1
  26.8 28.1 %all-gather.2.cloned.1.call-done = bf16[4096,256]{1,0:T(8,128)(2,1)} async-done(((bf16[256,256]{1,0:T(8,128)(2,1)}), bf16[4096,256]{1,0:T(8,128)(2,1)}) %all-gather.2.cloned.1.call-update) | async-done | bytes 2097168 | tf_op jit(solution)/shard_map/all_gather | solution.py:59
  54.9 4.1 gather_fusion
  59.0 5.9 %add_reduce_fusion.4 = (f32[24,256]{1,0:T(8,128)S(1)}, f32[24,256,256]{2,1,0:T(8,128)}) fusion(f32[24,256]{1,0:T(8,128)S(1)} %gather_fusion.2, bf16[24,256,256]{2,1,0:T(8,128)(2,1)} %gather_fusion, bf16[24,256,256]{2,1,0:T(8,128)(2,1)S(1)} %copy-done, pred[24]{0:T(512)(128)(4,1)S(1)} %iota_compare_fusion.2), kind=kOutput, calls=%fused_computation.27 | convolution fusion | flops 811591680 | bytes 12632088 | tf_op jit(solution)/shard_map/cbe,cde->cbd/dot_general | solution.py:72
  65.0 59.4 %pmax.42 = f32[16,256]{1,0:T(8,128)S(1)} all-reduce(f32[16,256]{1,0:T(8,128)S(1)} %select_reduce_fusion.2), channel_id=1, replica_groups=mesh['src'=2,'tgt'=16] {'tgt'}, use_global_device_ids=true, to_apply=%region_4.5 | all-reduce | flops 4096 | bytes 32768 | tf_op jit(solution)/shard_map/pmax | solution.py:38
  125.0 3.9 exponential_reduce_fusion.5
  129.2 57.6 %psum.42 = f32[16,256]{1,0:T(8,128)S(1)} all-reduce(f32[16,256]{1,0:T(8,128)S(1)} %fusion.10), channel_id=1, replica_groups=mesh['src'=2,'tgt'=16] {'tgt'}, use_global_device_ids=true, to_apply=%region_6.7 | all-reduce | flops 4096 | bytes 32768 | tf_op jit(solution)/shard_map/psum | solution.py:40
  187.4 3.4 add_reduce_fusion.3
  190.9 4.9 pmax.43
  196.4 3.6 exponential_reduce_fusion.4
  200.1 4.9 psum.43
  205.6 3.7 add_reduce_fusion.2
  209.4 57.6 %pmax.44 = f32[16,256]{1,0:T(8,128)S(1)} all-reduce(f32[16,256]{1,0:T(8,128)S(1)} %select_reduce_fusion.1), channel_id=1, replica_groups=mesh['src'=2,'tgt'=16] {'tgt'}, use_global_device_ids=true, to_apply=%region_14.15 | all-reduce | flops 4096 | bytes 32768 | tf_op jit(solution)/shard_map/pmax | solution.py:38
  267.6 3.9 exponential_reduce_fusion.3
  271.7 57.6 %psum.44 = f32[16,256]{1,0:T(8,128)S(1)} all-reduce(f32[16,256]{1,0:T(8,128)S(1)} %fusion.8), channel_id=1, replica_groups=mesh['src'=2,'tgt'=16] {'tgt'}, use_global_device_ids=true, to_apply=%region_16.17 | all-reduce | flops 4096 | bytes 32768 | tf_op jit(solution)/shard_map/psum | solution.py:40
  330.0 3.4 add_reduce_fusion.1
  333.4 4.9 pmax.45
  339.0 3.6 exponential_reduce_fusion.2
  342.6 4.9 psum.45
  348.2 3.7 add_reduce_fusion
  352.0 57.8 %pmax.46 = f32[16,256]{1,0:T(8,128)S(1)} all-reduce(f32[16,256]{1,0:T(8,128)S(1)} %select_reduce_fusion), channel_id=1, replica_groups=mesh['src'=2,'tgt'=16] {'tgt'}, use_global_device_ids=true, to_apply=%region_24.25 | all-reduce | flops 4096 | bytes 32768 | tf_op jit(solution)/shard_map/pmax | solution.py:38
  410.4 3.9 exponential_reduce_fusion.1
  414.5 57.6 %psum.46 = f32[16,256]{1,0:T(8,128)S(1)} all-reduce(f32[16,256]{1,0:T(8,128)S(1)} %fusion.6), channel_id=1, replica_groups=mesh['src'=2,'tgt'=16] {'tgt'}, use_global_device_ids=true, to_apply=%region_26.27 | all-reduce | flops 4096 | bytes 32768 | tf_op jit(solution)/shard_map/psum | solution.py:40
  472.7 3.4 add_reduce_fusion.5
  476.2 4.9 pmax.47
  481.7 3.6 exponential_reduce_fusion
  485.4 4.9 psum.47
  490.9 4.6 fusion
  (54 shorter events, 12.7 us)
Async XLA Ops:
  7.2 19.6 %copy-start.1 = (s32[1,1,24]{2,1,0:T(1,128)S(1)}, s32[1,1,24]{2,1,0:T(1,128)}, u32[]{:S(2)}) copy-start(s32[1,1,24]{2,1,0:T(1,128)} %param.8) | copy-start | bytes 292
  7.2 19.5 %copy-start.2 = (s32[1,1,24]{2,1,0:T(1,128)S(1)}, s32[1,1,24]{2,1,0:T(1,128)}, u32[]{:S(2)}) copy-start(s32[1,1,24]{2,1,0:T(1,128)} %param.7) | copy-start | bytes 292
  7.2 47.8 %all-gather.2.cloned.1.call-start = ((), (), s32[]{:S(2)}) async-start(), calls=%async_computation | async-start | bytes 2228224 | tf_op jit(solution)/shard_map/all_gather | solution.py:59
  25.9 33.2 %copy-start = (bf16[24,256,256]{2,1,0:T(8,128)(2,1)S(1)}, bf16[24,256,256]{2,1,0:T(8,128)(2,1)}, u32[]{:S(2)}) copy-start(bf16[24,256,256]{2,1,0:T(8,128)(2,1)} %gather_fusion.1) | copy-start | bytes 9437188
Sparse Core Ops, SparseCore 0:
  10.7 44.1 all-gather.1
where the time goes:
time: 504 us
  blocking collectives  387 us (77%)
  other arithmetic  51.9 us (10%)
  waiting for transfers between devices  28.1 us (6%)
  between operations  15.1 us (3%)
  local copies, waits for them, and re-layouts  14.3 us (3%)
  matrix products  7.02 us (1%)
    pmax x3, blocking collectives, row_potential(): top_value = lax.pmax(top_local, 'tgt')  175 us
    psum x3, blocking collectives, row_potential(): sum_total = lax.psum(spread_sum(slot_sums, row_hot), 'tgt')  173 us
    all_gather x1, waiting for transfers between devices, shards(): src_rows = lax.all_gather(unit_rows(src_emb), 'tgt', axis=0, tiled=True)  28.1 us
    pmax x3, blocking collectives, col_potential(): top_value = lax.pmax(top_local, 'src')  14.8 us
    psum x3, blocking collectives, col_potential(): sum_total = lax.psum(spread_sum(slot_sums, col_hot), 'src')  14.8 us
    reduce_sum x3, other arithmetic, row_potential(): jnp.sum(jnp.exp(shifted - top_value[rows_idx][:, :, None]), axis=2)  11.6 us
    reduce_sum x3, other arithmetic, col_potential(): jnp.sum(jnp.exp(shifted - top_value[cols_idx][:, None, :]), axis=1)  10.7 us
    reduce_max x3, other arithmetic, col_potential(): top_local = spread_top(jnp.max(shifted, axis=1), col_hot)  10.1 us
  transfers between devices with their start and end apart: 1, of which 1 were waited for; matrix products, arithmetic and copies ran while one was open for 1% of the time, Pallas kernels for 0%

commit v1 on v0

v1 whole, which is shorter than its diff:
```python
import functools
import math

import jax
import jax.numpy as jnp
from jax import lax
from jax.experimental import pallas as pl
from jax.experimental.pallas import tpu as pltpu
from jax.sharding import PartitionSpec as P

BLOCK = 256
ROW_BLOCKS = 16
COL_BLOCKS = 4
ITERS = 3
LANES = 128
SUB = 8

inv_temp = 250.0
sentinel = -1e30
log2e = math.log2(math.e)
ln2 = math.log(2.0)

VM = pl.BlockSpec(memory_space=pltpu.VMEM)
SM = pl.BlockSpec(memory_space=pltpu.SMEM)
ANY = pl.BlockSpec(memory_space=pl.ANY)


def unit_rows(embedding):
    values = embedding.astype(jnp.float32)
    inverse_norm = lax.rsqrt(jnp.sum(values * values, axis=1, keepdims=True) + 1e-06)
    return (values * inverse_norm).astype(jnp.bfloat16)


def swap(value, axis, key):
    size = lax.axis_size(axis)
    return lax.ppermute(value, axis, [(i, i ^ key) for i in range(size)])


def rounds_of(size):
    groups = []
    bit = 1
    while bit < size:
        if bit * 2 < size:
            groups.append((bit, 2 * bit, 3 * bit))
            bit *= 4
        else:
            groups.append((bit,))
            bit *= 2
    return groups


def merge_lse(parts):
    top = functools.reduce(jnp.maximum, parts)
    total = functools.reduce(jnp.add, [jnp.exp2(part - top) for part in parts])
    return top + jnp.log2(total)


def total_lse(local, axis):
    for keys in rounds_of(lax.axis_size(axis)):
        local = merge_lse([local] + [swap(local, axis, key) for key in keys])
    return local


def gather_rows(rows, axis):
    size = lax.axis_size(axis)
    groups = []
    bit = size
    held = [((0,), rows)]
    first = True
    while bit > 1:
        if first and bit >= 4:
            keys = (bit // 4, bit // 2, 3 * (bit // 4))
            bit //= 4
        else:
            keys = (bit // 2,)
            bit //= 2
        if first:
            news = [((key,), swap(rows, axis, key)) for key in keys]
            if len(news) > 1:
                news = [(sum((o for o, _ in news), ()), jnp.concatenate([r for _, r in news], 0))]
            first = False
        else:
            news = []
            for offsets, stack in held:
                for key in keys:
                    news.append((tuple(o ^ key for o in offsets), swap(stack, axis, key)))
        held = held + news
    return held


def first_pass_kernel(layout, share_src, share_tgt, meta, *refs):
    n_src, n_tgt = len(layout[0]), len(layout[1])
    src_parts = refs[:n_src]
    tgt_parts = refs[n_src : n_src + n_tgt]
    scores, lse, src_all, tgt_all, top, tot, sem = refs[n_src + n_tgt :]
    rows_at, cols_at, count, src_pos, tgt_pos = meta
    copies = []
    for parts, offsets_list, dest, pos, share in (
        (src_parts, layout[0], src_all, src_pos[0], share_src),
        (tgt_parts, layout[1], tgt_all, tgt_pos[0], share_tgt),
    ):
        for part, offsets in zip(parts, offsets_list):
            for k, offset in enumerate(offsets):
                start = pl.multiple_of((pos ^ offset) * share, share)
                copies.append(
                    pltpu.make_async_copy(
                        part.at[pl.ds(k * share, share)], dest.at[pl.ds(start, share)], sem.at[len(copies)]
                    )
                )
    for copy in copies:
        copy.start()
    top[...] = jnp.full(top.shape, sentinel, jnp.float32)
    tot[...] = jnp.zeros(tot.shape, jnp.float32)
    for copy in copies:
        copy.wait()

    def product(s):
        r = pl.multiple_of(rows_at[s] * BLOCK, BLOCK)
        c = pl.multiple_of(cols_at[s] * BLOCK, BLOCK)
        dot = lax.dot_general(
            tgt_all[pl.ds(c, BLOCK), :],
            src_all[pl.ds(r, BLOCK), :],
            (((1,), (1,)), ((), ())),
            preferred_element_type=jnp.float32,
        )
        scores[s] = dot * (inv_temp * log2e)

    def reduce(s):
        row_step(scores[s], rows_at[s], top, tot)

    n = count[0]
    product(0)

    def body(s, carry):
        product(s)
        reduce(s - 1)
        return carry

    lax.fori_loop(1, n, body, 0)
    reduce(n - 1)
    finish_rows(top, tot, lse)


def row_step(shifted, r, top, tot):
    tall = shifted.reshape(BLOCK // SUB, SUB, BLOCK)
    at = pl.ds(pl.multiple_of(r * SUB, SUB), SUB)
    old = top[at, :]
    new = jnp.maximum(old, jnp.max(tall, axis=0))
    sums = jnp.sum(jnp.exp2(tall - new[None]), axis=0)
    tot[at, :] = tot[at, :] * jnp.exp2(old - new) + sums
    top[at, :] = new


def finish_rows(top, tot, lse):
    tops = top[...].reshape(ROW_BLOCKS, SUB, BLOCK)
    best = jnp.max(tops, axis=1, keepdims=True)
    total = jnp.sum(tot[...].reshape(ROW_BLOCKS, SUB, BLOCK) * jnp.exp2(tops - best), axis=1)
    best = best.reshape(ROW_BLOCKS, BLOCK)
    lse[...] = jnp.where(best > 0.5 * sentinel, best + jnp.log2(total), sentinel)


def spread_cols(duals, wide):
    for n in range(COL_BLOCKS):
        wide[pl.ds(n * BLOCK, BLOCK), :] = jnp.broadcast_to(duals[n : n + 1, :], (LANES, BLOCK)).T


def row_kernel(meta, scores, cols, lse, wide, top, tot):
    rows_at, cols_at, count = meta
    top[...] = jnp.full(top.shape, sentinel, jnp.float32)
    tot[...] = jnp.zeros(tot.shape, jnp.float32)
    spread_cols(cols[...], wide)

    def body(s, carry):
        col = wide[pl.ds(pl.multiple_of(cols_at[s] * BLOCK, BLOCK), BLOCK), :]
        shifted = scores[s] + jnp.concatenate([col, col], axis=1)
        row_step(shifted, rows_at[s], top, tot)
        return carry

    lax.fori_loop(0, count[0], body, 0)
    finish_rows(top, tot, lse)


def col_kernel(meta, scores, rows, lse, top, tot):
    rows_at, cols_at, count = meta
    top[...] = jnp.full(top.shape, sentinel, jnp.float32)
    tot[...] = jnp.zeros(tot.shape, jnp.float32)

    def body(s, carry):
        at = pl.ds(pl.multiple_of(cols_at[s] * BLOCK, BLOCK), BLOCK)
        shifted = scores[s] + rows[pl.ds(rows_at[s], 1), :]
        low, high = shifted[:, :LANES], shifted[:, LANES:]
        old = top[at, :]
        new = jnp.maximum(old, jnp.maximum(low, high))
        tot[at, :] = tot[at, :] * jnp.exp2(old - new) + (jnp.exp2(low - new) + jnp.exp2(high - new))
        top[at, :] = new
        return carry

    lax.fori_loop(0, count[0], body, 0)
    tops = top[...].reshape(COL_BLOCKS, BLOCK, LANES)
    for n in range(COL_BLOCKS):
        flat = tops[n].T
        best = jnp.max(flat, axis=0, keepdims=True)
        total = jnp.sum(tot[pl.ds(n * BLOCK, BLOCK), :].T * jnp.exp2(flat - best), axis=0, keepdims=True)
        lse[pl.ds(n, 1), :] = best + jnp.log2(total)


def plan_kernel(meta, scores, rows, cols, out, wide, hold, sem):
    rows_at, cols_at, count = meta
    slots = out.shape[0]
    spread_cols(cols[...], wide)
    n = count[0]

    def put(s):
        return pltpu.make_async_copy(hold.at[s], out.at[s], sem)

    def body(s, carry):
        col = wide[pl.ds(pl.multiple_of(cols_at[s] * BLOCK, BLOCK), BLOCK), :]
        shifted = scores[s] + jnp.concatenate([col, col], axis=1) + rows[pl.ds(rows_at[s], 1), :]
        hold[s] = jnp.exp2(shifted).T.astype(jnp.bfloat16)
        put(s).start()
        return carry

    lax.fori_loop(0, n, body, 0)

    def blank(s, carry):
        hold[s] = jnp.zeros((BLOCK, BLOCK), jnp.bfloat16)
        put(s).start()
        return carry

    lax.fori_loop(n, slots, blank, 0)
    pltpu.make_async_copy(hold, out, sem).wait()


def split_meta(kernel, n_meta):
    def wrapped(*refs):
        return kernel(refs[:n_meta], *refs[n_meta:])

    return wrapped


def shards(src_emb, tgt_emb, block_rows, block_cols, block_counts):
    rows_at, cols_at = block_rows[0, 0], block_cols[0, 0]
    count = block_counts[0]
    slots = rows_at.shape[0]
    share_src, share_tgt = src_emb.shape[0], tgt_emb.shape[0]
    n_src, n_tgt = lax.axis_size("src"), lax.axis_size("tgt")
    src_unit, tgt_unit = unit_rows(src_emb), unit_rows(tgt_emb)
    src_held = gather_rows(src_unit, "tgt")
    tgt_held = gather_rows(tgt_unit, "src")
    layout = ([o for o, _ in src_held], [o for o, _ in tgt_held])
    pos = (lax.axis_index("tgt").reshape(1), lax.axis_index("src").reshape(1))
    meta = (rows_at, cols_at, count)
    f32 = jnp.float32
    wide = pltpu.VMEM((COL_BLOCKS * BLOCK, LANES), f32)
    row_acc = pltpu.VMEM((ROW_BLOCKS * SUB, BLOCK), f32)
    row_shape = jax.ShapeDtypeStruct((ROW_BLOCKS, BLOCK), f32)
    col_shape = jax.ShapeDtypeStruct((COL_BLOCKS, BLOCK), f32)
    n_copies = sum(len(o) for o in layout[0]) + sum(len(o) for o in layout[1])

    scores, lse = pl.pallas_call(
        split_meta(functools.partial(first_pass_kernel, layout, share_src, share_tgt), 5),
        in_specs=[SM] * 5 + [ANY] * (len(src_held) + len(tgt_held)),
        out_specs=[VM, VM],
        out_shape=[jax.ShapeDtypeStruct((slots, BLOCK, BLOCK), f32), row_shape],
        scratch_shapes=[
            pltpu.VMEM((ROW_BLOCKS * BLOCK, BLOCK), jnp.bfloat16),
            pltpu.VMEM((COL_BLOCKS * BLOCK, BLOCK), jnp.bfloat16),
            row_acc,
            row_acc,
            pltpu.SemaphoreType.DMA((n_copies,)),
        ],
        compiler_params=pltpu.CompilerParams(vmem_limit_bytes=24 << 20),
        name="first_rows",
    )(*meta, *pos, *[r for _, r in src_held], *[r for _, r in tgt_held])

    row_call = pl.pallas_call(
        split_meta(row_kernel, 3),
        in_specs=[SM] * 3 + [VM, VM],
        out_specs=VM,
        out_shape=row_shape,
        scratch_shapes=[wide, row_acc, row_acc],
        compiler_params=pltpu.CompilerParams(vmem_limit_bytes=24 << 20),
        name="rows",
    )
    col_call = pl.pallas_call(
        split_meta(col_kernel, 3),
        in_specs=[SM] * 3 + [VM, VM],
        out_specs=VM,
        out_shape=col_shape,
        scratch_shapes=[wide, wide],
        compiler_params=pltpu.CompilerParams(vmem_limit_bytes=24 << 20),
        name="cols",
    )
    log_ratio = math.log2(ROW_BLOCKS * n_src / (COL_BLOCKS * n_tgt))
    for sweep in range(ITERS):
        if sweep:
            lse = row_call(*meta, scores, col_dual)
        row_dual = -total_lse(lse, "tgt")
        col_dual = log_ratio - total_lse(col_call(*meta, scores, row_dual), "src")
    transport = pl.pallas_call(
        split_meta(plan_kernel, 3),
        in_specs=[SM] * 3 + [VM, VM, VM],
        out_specs=ANY,
        out_shape=jax.ShapeDtypeStruct((slots, BLOCK, BLOCK), jnp.bfloat16),
        scratch_shapes=[wide, pltpu.VMEM((slots, BLOCK, BLOCK), jnp.bfloat16), pltpu.SemaphoreType.DMA],
        compiler_params=pltpu.CompilerParams(vmem_limit_bytes=24 << 20),
        name="plan",
    )(*meta, scores, row_dual, col_dual)

    def own(dual, axis):
        width = dual.size // lax.axis_size(axis)
        part = lax.dynamic_slice_in_dim(dual.reshape(-1), lax.axis_index(axis) * width, width)
        return part * (ln2 / inv_temp)

    return (transport[None, None], own(row_dual, "tgt"), own(col_dual, "src"))


def solution(mesh):
    return jax.shard_map(
        shards,
        mesh=mesh,
        in_specs=(
            P(("src", "tgt"), None),
            P(("tgt", "src"), None),
            P("src", "tgt", None),
            P("src", "tgt", None),
            P("src", "tgt"),
        ),
        out_specs=(P("src", "tgt", None, None, None), P(("src", "tgt")), P(("tgt", "src"))),
        check_vma=False,
    )
```

time: 504 us -> 113 us (0.22)
  blocking collectives: 387 us -> 0 us
  other arithmetic: 51.9 us -> 5.77 us
  starting transfers between devices: 0.04 us -> 34.6 us
  Pallas kernels: 0 us -> 21.1 us
  waiting for transfers between devices: 28.1 us -> 45.4 us
  between operations: 15.1 us -> 1.55 us
  local copies, waits for them, and re-layouts: 14.3 us -> 4.15 us
  matrix products: 7.02 us -> 0 us
    pmax x6 -> x0, blocking collectives: 190 us -> none  [the longest x3 175 us: row_potential(): top_value = lax.pmax(top_local, 'tgt')]
    psum x6 -> x0, blocking collectives: 188 us -> none  [the longest x3 173 us: row_potential(): sum_total = lax.psum(spread_sum(slot_sums, row_hot), 'tgt')]
    ppermute x0 -> x31, waiting for transfers between devices: none -> 45.4 us  [swap(): return lax.ppermute(value, axis, [(i, i ^ key) for i in range(size)])]
    ppermute x0 -> x31, starting transfers between devices: none -> 34.6 us  [swap(): return lax.ppermute(value, axis, [(i, i ^ key) for i in range(size)])]
    all_gather x1 -> x0, waiting for transfers between devices: 28.1 us -> none  [shards(): src_rows = lax.all_gather(unit_rows(src_emb), 'tgt', axis=0, tiled=True)]
    reduce_sum x6 -> x0, other arithmetic: 22.3 us -> none  [the longest x3 11.6 us: row_potential(): jnp.sum(jnp.exp(shifted - top_value[rows_idx][:, :, None]), axis=2)]
    pallas_call x0 -> x7, Pallas kernels: none -> 21.1 us  [the longest x1 7.88 us: shards(): pl.pallas_call(split_meta(functools.partial(first_pass_kernel, layout, sh...]
    reduce_max x11 -> x0, other arithmetic: 18.1 us -> none  [the longest x3 10.1 us: col_potential(): top_local = spread_top(jnp.max(shifted, axis=1), col_hot)]
  transfers between devices with their start and end apart: 1 -> 31, of which waited for: 1 -> 23; matrix products, arithmetic and copies ran while one was open for 1% -> 3% of each run, Pallas kernels for 0% -> 0%
where the time goes in v1:
time: 113 us
  waiting for transfers between devices  45.4 us (40%)
  starting transfers between devices  34.6 us (31%)
  Pallas kernels  21.1 us (19%)
  other arithmetic  5.77 us (5%)
  local copies, waits for them, and re-layouts  4.15 us (4%)
  between operations  1.55 us (1%)
    ppermute x31, waiting for transfers between devices, swap(): return lax.ppermute(value, axis, [(i, i ^ key) for i in range(size)])  45.4 us
    ppermute x31, starting transfers between devices, swap(): return lax.ppermute(value, axis, [(i, i ^ key) for i in range(size)])  34.6 us
    pallas_call x1, Pallas kernels, shards(): pl.pallas_call(split_meta(functools.partial(first_pass_kernel, layout, sh...  7.88 us
    pallas_call x3, Pallas kernels, shards(): col_dual = log_ratio - total_lse(col_call(*meta, scores, row_dual), 'src')  5.82 us
    unnamed x16, local copies, waits for them, and re-layouts  4.14 us
    pallas_call x2, Pallas kernels, shards(): lse = row_call(*meta, scores, col_dual)  3.91 us
    pallas_call x1, Pallas kernels, shards(): pl.pallas_call(split_meta(plan_kernel, 3), in_specs=[SM] * 3 + [VM, VM, V...  3.54 us
  transfers between devices with their start and end apart: 31, of which 23 were waited for; matrix products, arithmetic and copies ran while one was open for 3% of the time, Pallas kernels for 0%

profile of v1, /device:TPU:0, one launch (start us, length us, event | category | flops | bytes accessed | tf_op | source)
XLA Modules:
  0.0 112.6 jit_solution(809301026558418195)
XLA Ops:
  2.7 3.1 %collective-permute-start = (bf16[256,256]{1,0:T(8,128)(2,1)S(1)}, bf16[256,256]{1,0:T(8,128)(2,1)S(1)}, u32[]{:S(2)}, u32[]{:S(2)}) collective-permute-start(bf16[256,256]{1,0:T(8,128)(2,1)S(1)} %fusion.3.refs_5_), channel_id=1, source_target_pairs={{0,4},{1,5},{2,6},{3,7},{4,0},{5,1},{6,2},{7,3},{8,12},{9,13},{10,... | collective-permute-start | bytes 393224 | tf_op jit(solution)/shard_map/ppermute | solution.py:36
  5.8 2.6 %collective-permute-start.1 = (bf16[256,256]{1,0:T(8,128)(2,1)S(1)}, bf16[256,256]{1,0:T(8,128)(2,1)S(1)}, u32[]{:S(2)}, u32[]{:S(2)}) collective-permute-start(bf16[256,256]{1,0:T(8,128)(2,1)S(1)} %fusion.3.refs_5_), channel_id=1, source_target_pairs={{0,8},{1,9},{2,10},{3,11},{4,12},{5,13},{6,14},{7,15},{8,0},{9,1},... | collective-permute-start | bytes 393224 | tf_op jit(solution)/shard_map/ppermute | solution.py:36
  8.4 2.5 %collective-permute-done = bf16[256,256]{1,0:T(8,128)(2,1)S(1)} collective-permute-done((bf16[256,256]{1,0:T(8,128)(2,1)S(1)}, bf16[256,256]{1,0:T(8,128)(2,1)S(1)}, u32[]{:S(2)}, u32[]{:S(2)}) %collective-permute-start) | collective-permute-done | bytes 131104 | tf_op jit(solution)/shard_map/ppermute | solution.py:36
  10.9 7.8 %collective-permute-done.1 = bf16[256,256]{1,0:T(8,128)(2,1)S(1)} collective-permute-done((bf16[256,256]{1,0:T(8,128)(2,1)S(1)}, bf16[256,256]{1,0:T(8,128)(2,1)S(1)}, u32[]{:S(2)}, u32[]{:S(2)}) %collective-permute-start.1) | collective-permute-done | bytes 131104 | tf_op jit(solution)/shard_map/ppermute | solution.py:36
  18.7 1.6 %collective-permute-start.4 = (bf16[768,256]{1,0:T(8,128)(2,1)S(1)}, bf16[768,256]{1,0:T(8,128)(2,1)S(1)}, u32[]{:S(2)}, u32[]{:S(2)}) collective-permute-start(bf16[768,256]{1,0:T(8,128)(2,1)S(1)} %constant_dynamic-update-slice_fusion.refs_6_), channel_id=1, source_target_pairs={{0,2},{1,3},{2,0},{3,1},{4,6},{5,7},{6,4},{7,5},{8,10},{9,11},{10,... | collective-permute-start | bytes 1179656 | tf_op jit(solution)/shard_map/ppermute | solution.py:36
  22.0 6.6 %collective-permute-done.4.refs_8_ = bf16[768,256]{1,0:T(8,128)(2,1)S(1)} collective-permute-done((bf16[768,256]{1,0:T(8,128)(2,1)S(1)}, bf16[768,256]{1,0:T(8,128)(2,1)S(1)}, u32[]{:S(2)}, u32[]{:S(2)}) %collective-permute-start.4) | collective-permute-done | bytes 393248 | tf_op jit(solution)/shard_map/ppermute | solution.py:36
  29.7 1.6 %collective-permute-start.9 = (bf16[512,256]{1,0:T(8,128)(2,1)S(1)}, bf16[512,256]{1,0:T(8,128)(2,1)S(1)}, u32[]{:S(2)}, u32[]{:S(2)}) collective-permute-start(bf16[512,256]{1,0:T(8,128)(2,1)S(1)} %fusion.1.refs_13_), channel_id=1, source_target_pairs={{0,16},{16,0},{1,17},{17,1},{2,18},{18,2},{3,19},{19,3},{4,20},{20... | collective-permute-start | bytes 786440 | tf_op jit(solution)/shard_map/ppermute | solution.py:36
  32.9 5.6 %collective-permute-done.9.refs_14_ = bf16[512,256]{1,0:T(8,128)(2,1)S(1)} collective-permute-done((bf16[512,256]{1,0:T(8,128)(2,1)S(1)}, bf16[512,256]{1,0:T(8,128)(2,1)S(1)}, u32[]{:S(2)}, u32[]{:S(2)}) %collective-permute-start.9) | collective-permute-done | bytes 262176 | tf_op jit(solution)/shard_map/ppermute | solution.py:36
  39.8 7.9 %first_rows.1 = (f32[24,256,256]{2,1,0:T(8,128)S(1)}, f32[16,256]{1,0:T(8,128)S(1)}) custom-call(s32[24]{0:T(128)S(1)} %bitcast.19, s32[24]{0:T(128)S(1)} %bitcast.26, s32[1]{0:T(128)} %bitcast.10.refs_2_, s32[1]{0:T(128)} %bitcast.3.refs_3_, s32[1]{0:T(128)} %bitcast.4.refs_4_, bf16[256,256]{1,0:T(8,128)(2,1)S(1)} %fusion.3.refs_5_, ...), custom_call_target="tpu_custom_call" | custom-call | tf_op jit(solution)/shard_map/first_rows/pallas_call | solution.py:260
  49.6 1.3 %collective-permute-done.12 = f32[16,256]{1,0:T(8,128)S(1)} collective-permute-done((f32[16,256]{1,0:T(8,128)S(1)}, f32[16,256]{1,0:T(8,128)S(1)}, u32[]{:S(2)}, u32[]{:S(2)}) %collective-permute-start.12) | collective-permute-done | bytes 16416 | tf_op jit(solution)/shard_map/ppermute | solution.py:36
  52.3 7.2 %collective-permute-start.14 = (f32[16,256]{1,0:T(8,128)S(1)}, f32[16,256]{1,0:T(8,128)S(1)}, u32[]{:S(2)}, u32[]{:S(2)}) collective-permute-start(f32[16,256]{1,0:T(8,128)S(1)} %multiply_add_fusion.2), channel_id=1, source_target_pairs={{0,8},{1,9},{2,10},{3,11},{4,12},{5,13},{6,14},{7,15},{8,0},{9,1},... | collective-permute-start | bytes 49160 | tf_op jit(solution)/shard_map/ppermute | solution.py:36
  60.1 1.3 %collective-permute-done.14 = f32[16,256]{1,0:T(8,128)S(1)} collective-permute-done((f32[16,256]{1,0:T(8,128)S(1)}, f32[16,256]{1,0:T(8,128)S(1)}, u32[]{:S(2)}, u32[]{:S(2)}) %collective-permute-start.14) | collective-permute-done | bytes 16416 | tf_op jit(solution)/shard_map/ppermute | solution.py:36
  61.4 1.9 %collective-permute-done.13 = f32[16,256]{1,0:T(8,128)S(1)} collective-permute-done((f32[16,256]{1,0:T(8,128)S(1)}, f32[16,256]{1,0:T(8,128)S(1)}, u32[]{:S(2)}, u32[]{:S(2)}) %collective-permute-start.13) | collective-permute-done | bytes 16416 | tf_op jit(solution)/shard_map/ppermute | solution.py:36
  63.3 1.9 %cols.3 = f32[4,256]{1,0:T(4,128)S(1)} custom-call(s32[24]{0:T(128)S(1)} %bitcast.20, s32[24]{0:T(128)S(1)} %bitcast.27, s32[1]{0:T(128)} %bitcast.11.refs_2_, f32[24,256,256]{2,1,0:T(8,128)S(1)} %get-tuple-element.5.refs_3_, f32[16,256]{1,0:T(8,128)S(1)} %add_negate_fusion.2.refs_4_), custom_call_target="tpu_custom_call" | custom-call | tf_op jit(solution)/shard_map/cols/pallas_call | solution.py:299
  65.4 3.6 %collective-permute-done.16 = f32[4,256]{1,0:T(4,128)S(1)} collective-permute-done((f32[4,256]{1,0:T(4,128)S(1)}, f32[4,256]{1,0:T(4,128)S(1)}, u32[]{:S(2)}, u32[]{:S(2)}) %collective-permute-start.16) | collective-permute-done | bytes 4128 | tf_op jit(solution)/shard_map/ppermute | solution.py:36
  69.0 2.0 %rows.2 = f32[16,256]{1,0:T(8,128)S(1)} custom-call(s32[24]{0:T(128)S(1)} %bitcast.21, s32[24]{0:T(128)S(1)} %bitcast.28, s32[1]{0:T(128)} %bitcast.12.refs_2_, f32[24,256,256]{2,1,0:T(8,128)S(1)} %get-tuple-element.5.refs_3_, f32[4,256]{1,0:T(4,128)S(1)} %add_subtract_fusion.2.refs_4_), custom_call_target="tpu_custom_call" | custom-call | tf_op jit(solution)/shard_map/rows/pallas_call | solution.py:297
  71.6 1.3 %collective-permute-start.17 = (f32[16,256]{1,0:T(8,128)S(1)}, f32[16,256]{1,0:T(8,128)S(1)}, u32[]{:S(2)}, u32[]{:S(2)}) collective-permute-start(f32[16,256]{1,0:T(8,128)S(1)} %rows.2), channel_id=1, source_target_pairs={{0,1},{1,0},{2,3},{3,2},{4,5},{5,4},{6,7},{7,6},{8,9},{9,8},{10,11... | collective-permute-start | bytes 49160 | tf_op jit(solution)/shard_map/ppermute | solution.py:36
  72.9 1.3 %collective-permute-done.19 = f32[16,256]{1,0:T(8,128)S(1)} collective-permute-done((f32[16,256]{1,0:T(8,128)S(1)}, f32[16,256]{1,0:T(8,128)S(1)}, u32[]{:S(2)}, u32[]{:S(2)}) %collective-permute-start.19) | collective-permute-done | bytes 16416 | tf_op jit(solution)/shard_map/ppermute | solution.py:36
  74.9 1.9 %collective-permute-start.22 = (f32[16,256]{1,0:T(8,128)S(1)}, f32[16,256]{1,0:T(8,128)S(1)}, u32[]{:S(2)}, u32[]{:S(2)}) collective-permute-start(f32[16,256]{1,0:T(8,128)S(1)} %multiply_add_fusion.1), channel_id=1, source_target_pairs={{0,12},{1,13},{2,14},{3,15},{4,8},{5,9},{6,10},{7,11},{8,4},{9,5},... | collective-permute-start | bytes 49160 | tf_op jit(solution)/shard_map/ppermute | solution.py:36
  77.8 1.5 %collective-permute-start.20 = (f32[16,256]{1,0:T(8,128)S(1)}, f32[16,256]{1,0:T(8,128)S(1)}, u32[]{:S(2)}, u32[]{:S(2)}) collective-permute-start(f32[16,256]{1,0:T(8,128)S(1)} %multiply_add_fusion.1), channel_id=1, source_target_pairs={{0,4},{1,5},{2,6},{3,7},{4,0},{5,1},{6,2},{7,3},{8,12},{9,13},{10,... | collective-permute-start | bytes 49160 | tf_op jit(solution)/shard_map/ppermute | solution.py:36
  81.6 1.9 %cols.4 = f32[4,256]{1,0:T(4,128)S(1)} custom-call(s32[24]{0:T(128)S(1)} %bitcast.22, s32[24]{0:T(128)S(1)} %bitcast.29, s32[1]{0:T(128)} %bitcast.13.refs_2_, f32[24,256,256]{2,1,0:T(8,128)S(1)} %get-tuple-element.5.refs_3_, f32[16,256]{1,0:T(8,128)S(1)} %add_negate_fusion.1.refs_4_), custom_call_target="tpu_custom_call" | custom-call | tf_op jit(solution)/shard_map/cols/pallas_call | solution.py:299
  84.2 3.0 %collective-permute-done.23 = f32[4,256]{1,0:T(4,128)S(1)} collective-permute-done((f32[4,256]{1,0:T(4,128)S(1)}, f32[4,256]{1,0:T(4,128)S(1)}, u32[]{:S(2)}, u32[]{:S(2)}) %collective-permute-start.23) | collective-permute-done | bytes 4128 | tf_op jit(solution)/shard_map/ppermute | solution.py:36
  87.2 2.0 %rows.3 = f32[16,256]{1,0:T(8,128)S(1)} custom-call(s32[24]{0:T(128)S(1)} %bitcast.23, s32[24]{0:T(128)S(1)} %bitcast.30, s32[1]{0:T(128)} %bitcast.14.refs_2_, f32[24,256,256]{2,1,0:T(8,128)S(1)} %get-tuple-element.5.refs_3_, f32[4,256]{1,0:T(4,128)S(1)} %add_subtract_fusion.1.refs_4_), custom_call_target="tpu_custom_call" | custom-call | tf_op jit(solution)/shard_map/rows/pallas_call | solution.py:297
  89.4 1.8 %collective-permute-start.24 = (f32[16,256]{1,0:T(8,128)S(1)}, f32[16,256]{1,0:T(8,128)S(1)}, u32[]{:S(2)}, u32[]{:S(2)}) collective-permute-start(f32[16,256]{1,0:T(8,128)S(1)} %rows.3), channel_id=1, source_target_pairs={{0,1},{1,0},{2,3},{3,2},{4,5},{5,4},{6,7},{7,6},{8,9},{9,8},{10,11... | collective-permute-start | bytes 49160 | tf_op jit(solution)/shard_map/ppermute | solution.py:36
  91.1 1.3 %collective-permute-done.26 = f32[16,256]{1,0:T(8,128)S(1)} collective-permute-done((f32[16,256]{1,0:T(8,128)S(1)}, f32[16,256]{1,0:T(8,128)S(1)}, u32[]{:S(2)}, u32[]{:S(2)}) %collective-permute-start.26) | collective-permute-done | bytes 16416 | tf_op jit(solution)/shard_map/ppermute | solution.py:36
  94.1 2.1 %collective-permute-start.28 = (f32[16,256]{1,0:T(8,128)S(1)}, f32[16,256]{1,0:T(8,128)S(1)}, u32[]{:S(2)}, u32[]{:S(2)}) collective-permute-start(f32[16,256]{1,0:T(8,128)S(1)} %multiply_add_fusion), channel_id=1, source_target_pairs={{0,8},{1,9},{2,10},{3,11},{4,12},{5,13},{6,14},{7,15},{8,0},{9,1},... | collective-permute-start | bytes 49160 | tf_op jit(solution)/shard_map/ppermute | solution.py:36
  96.2 1.4 %collective-permute-start.27 = (f32[16,256]{1,0:T(8,128)S(1)}, f32[16,256]{1,0:T(8,128)S(1)}, u32[]{:S(2)}, u32[]{:S(2)}) collective-permute-start(f32[16,256]{1,0:T(8,128)S(1)} %multiply_add_fusion), channel_id=1, source_target_pairs={{0,4},{1,5},{2,6},{3,7},{4,0},{5,1},{6,2},{7,3},{8,12},{9,13},{10,... | collective-permute-start | bytes 49160 | tf_op jit(solution)/shard_map/ppermute | solution.py:36
  97.6 1.2 %collective-permute-done.29 = f32[16,256]{1,0:T(8,128)S(1)} collective-permute-done((f32[16,256]{1,0:T(8,128)S(1)}, f32[16,256]{1,0:T(8,128)S(1)}, u32[]{:S(2)}, u32[]{:S(2)}) %collective-permute-start.29) | collective-permute-done | bytes 16416 | tf_op jit(solution)/shard_map/ppermute | solution.py:36
  100.0 2.8 %copy-done.1 = f32[24,256,256]{2,1,0:T(8,128)S(1)} copy-done((f32[24,256,256]{2,1,0:T(8,128)S(1)}, f32[24,256,256]{2,1,0:T(8,128)}, u32[]{:S(2)}) %copy-start.1) | copy-done | bytes 6291480
  102.7 2.0 %cols.5 = f32[4,256]{1,0:T(4,128)S(1)} custom-call(s32[24]{0:T(128)S(1)} %bitcast.24, s32[24]{0:T(128)S(1)} %bitcast.31, s32[1]{0:T(128)} %bitcast.15.refs_2_, f32[24,256,256]{2,1,0:T(8,128)S(1)} %copy-done.1, f32[16,256]{1,0:T(8,128)S(1)} %add_negate_fusion.refs_4_), custom_call_target="tpu_custom_call" | custom-call | tf_op jit(solution)/shard_map/cols/pallas_call | solution.py:299
  106.3 2.1 %collective-permute-done.30 = f32[4,256]{1,0:T(4,128)S(1)} collective-permute-done((f32[4,256]{1,0:T(4,128)S(1)}, f32[4,256]{1,0:T(4,128)S(1)}, u32[]{:S(2)}, u32[]{:S(2)}) %collective-permute-start.30) | collective-permute-done | bytes 4128 | tf_op jit(solution)/shard_map/ppermute | solution.py:36
  108.4 3.5 %plan.1 = bf16[24,256,256]{2,1,0:T(8,128)(2,1)} custom-call(s32[24]{0:T(128)S(1)} %bitcast.25, s32[24]{0:T(128)S(1)} %bitcast.32, s32[1]{0:T(128)} %bitcast.16.refs_2_, f32[24,256,256]{2,1,0:T(8,128)S(1)} %copy-done.1, f32[16,256]{1,0:T(8,128)S(1)} %add_negate_fusion.refs_4_, f32[4,256]{1,0:T(4,128)S(1)} %add_subtract_fusion.refs_5_), custom_call_target="tpu_custom_call" | custom-call | tf_op jit(solution)/shard_map/plan/pallas_call | solution.py:300
  (71 shorter events, 21.5 us)
Async XLA Ops:
  2.7 8.2 %collective-permute-start = (bf16[256,256]{1,0:T(8,128)(2,1)S(1)}, bf16[256,256]{1,0:T(8,128)(2,1)S(1)}, u32[]{:S(2)}, u32[]{:S(2)}) collective-permute-start(bf16[256,256]{1,0:T(8,128)(2,1)S(1)} %fusion.3.refs_5_), channel_id=1, source_target_pairs={{0,4},{1,5},{2,6},{3,7},{4,0},{5,1},{6,2},{7,3},{8,12},{9,13},{10,... | collective-permute-start | bytes 393224 | tf_op jit(solution)/shard_map/ppermute | solution.py:36
  5.8 12.9 %collective-permute-start.1 = (bf16[256,256]{1,0:T(8,128)(2,1)S(1)}, bf16[256,256]{1,0:T(8,128)(2,1)S(1)}, u32[]{:S(2)}, u32[]{:S(2)}) collective-permute-start(bf16[256,256]{1,0:T(8,128)(2,1)S(1)} %fusion.3.refs_5_), channel_id=1, source_target_pairs={{0,8},{1,9},{2,10},{3,11},{4,12},{5,13},{6,14},{7,15},{8,0},{9,1},... | collective-permute-start | bytes 393224 | tf_op jit(solution)/shard_map/ppermute | solution.py:36
  8.4 10.3 %collective-permute-start.2 = (bf16[256,256]{1,0:T(8,128)(2,1)S(1)}, bf16[256,256]{1,0:T(8,128)(2,1)S(1)}, u32[]{:S(2)}, u32[]{:S(2)}) collective-permute-start(bf16[256,256]{1,0:T(8,128)(2,1)S(1)} %fusion.3.refs_5_), channel_id=1, source_target_pairs={{0,12},{1,13},{2,14},{3,15},{4,8},{5,9},{6,10},{7,11},{8,4},{9,5},... | collective-permute-start | bytes 393224 | tf_op jit(solution)/shard_map/ppermute | solution.py:36
  18.7 9.9 %collective-permute-start.4 = (bf16[768,256]{1,0:T(8,128)(2,1)S(1)}, bf16[768,256]{1,0:T(8,128)(2,1)S(1)}, u32[]{:S(2)}, u32[]{:S(2)}) collective-permute-start(bf16[768,256]{1,0:T(8,128)(2,1)S(1)} %constant_dynamic-update-slice_fusion.refs_6_), channel_id=1, source_target_pairs={{0,2},{1,3},{2,0},{3,1},{4,6},{5,7},{6,4},{7,5},{8,10},{9,11},{10,... | collective-permute-start | bytes 1179656 | tf_op jit(solution)/shard_map/ppermute | solution.py:36
  20.3 11.2 %collective-permute-start.3 = (bf16[256,256]{1,0:T(8,128)(2,1)S(1)}, bf16[256,256]{1,0:T(8,128)(2,1)S(1)}, u32[]{:S(2)}, u32[]{:S(2)}) collective-permute-start(bf16[256,256]{1,0:T(8,128)(2,1)S(1)} %fusion.3.refs_5_), channel_id=1, source_target_pairs={{0,2},{1,3},{2,0},{3,1},{4,6},{5,7},{6,4},{7,5},{8,10},{9,11},{10,... | collective-permute-start | bytes 393224 | tf_op jit(solution)/shard_map/ppermute | solution.py:36
  21.9 16.6 %collective-permute-start.6 = (bf16[768,256]{1,0:T(8,128)(2,1)S(1)}, bf16[768,256]{1,0:T(8,128)(2,1)S(1)}, u32[]{:S(2)}, u32[]{:S(2)}) collective-permute-start(bf16[768,256]{1,0:T(8,128)(2,1)S(1)} %constant_dynamic-update-slice_fusion.refs_6_), channel_id=1, source_target_pairs={{0,1},{1,0},{2,3},{3,2},{4,5},{5,4},{6,7},{7,6},{8,9},{9,8},{10,11... | collective-permute-start | bytes 1179656 | tf_op jit(solution)/shard_map/ppermute | solution.py:36
  28.6 9.9 %collective-permute-start.8 = (bf16[768,256]{1,0:T(8,128)(2,1)S(1)}, bf16[768,256]{1,0:T(8,128)(2,1)S(1)}, u32[]{:S(2)}, u32[]{:S(2)}) collective-permute-start(bf16[768,256]{1,0:T(8,128)(2,1)S(1)} %collective-permute-done.4.refs_8_), channel_id=1, source_target_pairs={{0,1},{1,0},{2,3},{3,2},{4,5},{5,4},{6,7},{7,6},{8,9},{9,8},{10,11... | collective-permute-start | bytes 1179656 | tf_op jit(solution)/shard_map/ppermute | solution.py:36
  29.7 8.8 %collective-permute-start.9 = (bf16[512,256]{1,0:T(8,128)(2,1)S(1)}, bf16[512,256]{1,0:T(8,128)(2,1)S(1)}, u32[]{:S(2)}, u32[]{:S(2)}) collective-permute-start(bf16[512,256]{1,0:T(8,128)(2,1)S(1)} %fusion.1.refs_13_), channel_id=1, source_target_pairs={{0,16},{16,0},{1,17},{17,1},{2,18},{18,2},{3,19},{19,3},{4,20},{20... | collective-permute-start | bytes 786440 | tf_op jit(solution)/shard_map/ppermute | solution.py:36
  31.3 1.3 %collective-permute-start.5 = (bf16[256,256]{1,0:T(8,128)(2,1)S(1)}, bf16[256,256]{1,0:T(8,128)(2,1)S(1)}, u32[]{:S(2)}, u32[]{:S(2)}) collective-permute-start(bf16[256,256]{1,0:T(8,128)(2,1)S(1)} %fusion.3.refs_5_), channel_id=1, source_target_pairs={{0,1},{1,0},{2,3},{3,2},{4,5},{5,4},{6,7},{7,6},{8,9},{9,8},{10,11... | collective-permute-start | bytes 393224 | tf_op jit(solution)/shard_map/ppermute | solution.py:36
  31.5 1.3 %collective-permute-start.7 = (bf16[256,256]{1,0:T(8,128)(2,1)S(1)}, bf16[256,256]{1,0:T(8,128)(2,1)S(1)}, u32[]{:S(2)}, u32[]{:S(2)}) collective-permute-start(bf16[256,256]{1,0:T(8,128)(2,1)S(1)} %collective-permute-done.3.refs_7_), channel_id=1, source_target_pairs={{0,1},{1,0},{2,3},{3,2},{4,5},{5,4},{6,7},{7,6},{8,9},{9,8},{10,11... | collective-permute-start | bytes 393224 | tf_op jit(solution)/shard_map/ppermute | solution.py:36
  47.7 39.5 %copy-start = (f32[24,256,256]{2,1,0:T(8,128)}, f32[24,256,256]{2,1,0:T(8,128)S(1)}, u32[]{:S(2)}) copy-start(f32[24,256,256]{2,1,0:T(8,128)S(1)} %get-tuple-element.5.refs_3_) | copy-start | bytes 18874372
  47.7 3.2 %collective-permute-start.12 = (f32[16,256]{1,0:T(8,128)S(1)}, f32[16,256]{1,0:T(8,128)S(1)}, u32[]{:S(2)}, u32[]{:S(2)}) collective-permute-start(f32[16,256]{1,0:T(8,128)S(1)} %get-tuple-element.6), channel_id=1, source_target_pairs={{0,3},{1,2},{2,1},{3,0},{4,7},{5,6},{6,5},{7,4},{8,11},{9,10},{10,... | collective-permute-start | bytes 49160 | tf_op jit(solution)/shard_map/ppermute | solution.py:36
  47.8 3.8 %collective-permute-start.11 = (f32[16,256]{1,0:T(8,128)S(1)}, f32[16,256]{1,0:T(8,128)S(1)}, u32[]{:S(2)}, u32[]{:S(2)}) collective-permute-start(f32[16,256]{1,0:T(8,128)S(1)} %get-tuple-element.6), channel_id=1, source_target_pairs={{0,2},{1,3},{2,0},{3,1},{4,6},{5,7},{6,4},{7,5},{8,10},{9,11},{10,... | collective-permute-start | bytes 49160 | tf_op jit(solution)/shard_map/ppermute | solution.py:36
  48.5 3.1 %collective-permute-start.10 = (f32[16,256]{1,0:T(8,128)S(1)}, f32[16,256]{1,0:T(8,128)S(1)}, u32[]{:S(2)}, u32[]{:S(2)}) collective-permute-start(f32[16,256]{1,0:T(8,128)S(1)} %get-tuple-element.6), channel_id=1, source_target_pairs={{0,1},{1,0},{2,3},{3,2},{4,5},{5,4},{6,7},{7,6},{8,9},{9,8},{10,11... | collective-permute-start | bytes 49160 | tf_op jit(solution)/shard_map/ppermute | solution.py:36
  51.6 8.4 %collective-permute-start.15 = (f32[16,256]{1,0:T(8,128)S(1)}, f32[16,256]{1,0:T(8,128)S(1)}, u32[]{:S(2)}, u32[]{:S(2)}) collective-permute-start(f32[16,256]{1,0:T(8,128)S(1)} %multiply_add_fusion.2), channel_id=1, source_target_pairs={{0,12},{1,13},{2,14},{3,15},{4,8},{5,9},{6,10},{7,11},{8,4},{9,5},... | collective-permute-start | bytes 49160 | tf_op jit(solution)/shard_map/ppermute | solution.py:36
  52.3 9.1 %collective-permute-start.14 = (f32[16,256]{1,0:T(8,128)S(1)}, f32[16,256]{1,0:T(8,128)S(1)}, u32[]{:S(2)}, u32[]{:S(2)}) collective-permute-start(f32[16,256]{1,0:T(8,128)S(1)} %multiply_add_fusion.2), channel_id=1, source_target_pairs={{0,8},{1,9},{2,10},{3,11},{4,12},{5,13},{6,14},{7,15},{8,0},{9,1},... | collective-permute-start | bytes 49160 | tf_op jit(solution)/shard_map/ppermute | solution.py:36
  59.6 3.7 %collective-permute-start.13 = (f32[16,256]{1,0:T(8,128)S(1)}, f32[16,256]{1,0:T(8,128)S(1)}, u32[]{:S(2)}, u32[]{:S(2)}) collective-permute-start(f32[16,256]{1,0:T(8,128)S(1)} %multiply_add_fusion.2), channel_id=1, source_target_pairs={{0,4},{1,5},{2,6},{3,7},{4,0},{5,1},{6,2},{7,3},{8,12},{9,13},{10,... | collective-permute-start | bytes 49160 | tf_op jit(solution)/shard_map/ppermute | solution.py:36
  65.3 3.7 %collective-permute-start.16 = (f32[4,256]{1,0:T(4,128)S(1)}, f32[4,256]{1,0:T(4,128)S(1)}, u32[]{:S(2)}, u32[]{:S(2)}) collective-permute-start(f32[4,256]{1,0:T(4,128)S(1)} %cols.3), channel_id=1, source_target_pairs={{0,16},{16,0},{1,17},{17,1},{2,18},{18,2},{3,19},{19,3},{4,20},{20... | collective-permute-start | bytes 12296 | tf_op jit(solution)/shard_map/ppermute | solution.py:36
  70.9 3.2 %collective-permute-start.19 = (f32[16,256]{1,0:T(8,128)S(1)}, f32[16,256]{1,0:T(8,128)S(1)}, u32[]{:S(2)}, u32[]{:S(2)}) collective-permute-start(f32[16,256]{1,0:T(8,128)S(1)} %rows.2), channel_id=1, source_target_pairs={{0,3},{1,2},{2,1},{3,0},{4,7},{5,6},{6,5},{7,4},{8,11},{9,10},{10,... | collective-permute-start | bytes 49160 | tf_op jit(solution)/shard_map/ppermute | solution.py:36
  71.0 3.8 %collective-permute-start.18 = (f32[16,256]{1,0:T(8,128)S(1)}, f32[16,256]{1,0:T(8,128)S(1)}, u32[]{:S(2)}, u32[]{:S(2)}) collective-permute-start(f32[16,256]{1,0:T(8,128)S(1)} %rows.2), channel_id=1, source_target_pairs={{0,2},{1,3},{2,0},{3,1},{4,6},{5,7},{6,4},{7,5},{8,10},{9,11},{10,... | collective-permute-start | bytes 49160 | tf_op jit(solution)/shard_map/ppermute | solution.py:36
  71.6 3.2 %collective-permute-start.17 = (f32[16,256]{1,0:T(8,128)S(1)}, f32[16,256]{1,0:T(8,128)S(1)}, u32[]{:S(2)}, u32[]{:S(2)}) collective-permute-start(f32[16,256]{1,0:T(8,128)S(1)} %rows.2), channel_id=1, source_target_pairs={{0,1},{1,0},{2,3},{3,2},{4,5},{5,4},{6,7},{7,6},{8,9},{9,8},{10,11... | collective-permute-start | bytes 49160 | tf_op jit(solution)/shard_map/ppermute | solution.py:36
  74.9 5.6 %collective-permute-start.22 = (f32[16,256]{1,0:T(8,128)S(1)}, f32[16,256]{1,0:T(8,128)S(1)}, u32[]{:S(2)}, u32[]{:S(2)}) collective-permute-start(f32[16,256]{1,0:T(8,128)S(1)} %multiply_add_fusion.1), channel_id=1, source_target_pairs={{0,12},{1,13},{2,14},{3,15},{4,8},{5,9},{6,10},{7,11},{8,4},{9,5},... | collective-permute-start | bytes 49160 | tf_op jit(solution)/shard_map/ppermute | solution.py:36
  76.7 4.6 %collective-permute-start.21 = (f32[16,256]{1,0:T(8,128)S(1)}, f32[16,256]{1,0:T(8,128)S(1)}, u32[]{:S(2)}, u32[]{:S(2)}) collective-permute-start(f32[16,256]{1,0:T(8,128)S(1)} %multiply_add_fusion.1), channel_id=1, source_target_pairs={{0,8},{1,9},{2,10},{3,11},{4,12},{5,13},{6,14},{7,15},{8,0},{9,1},... | collective-permute-start | bytes 49160 | tf_op jit(solution)/shard_map/ppermute | solution.py:36
  77.8 3.8 %collective-permute-start.20 = (f32[16,256]{1,0:T(8,128)S(1)}, f32[16,256]{1,0:T(8,128)S(1)}, u32[]{:S(2)}, u32[]{:S(2)}) collective-permute-start(f32[16,256]{1,0:T(8,128)S(1)} %multiply_add_fusion.1), channel_id=1, source_target_pairs={{0,4},{1,5},{2,6},{3,7},{4,0},{5,1},{6,2},{7,3},{8,12},{9,13},{10,... | collective-permute-start | bytes 49160 | tf_op jit(solution)/shard_map/ppermute | solution.py:36
  83.5 3.7 %collective-permute-start.23 = (f32[4,256]{1,0:T(4,128)S(1)}, f32[4,256]{1,0:T(4,128)S(1)}, u32[]{:S(2)}, u32[]{:S(2)}) collective-permute-start(f32[4,256]{1,0:T(4,128)S(1)} %cols.4), channel_id=1, source_target_pairs={{0,16},{16,0},{1,17},{17,1},{2,18},{18,2},{3,19},{19,3},{4,20},{20... | collective-permute-start | bytes 12296 | tf_op jit(solution)/shard_map/ppermute | solution.py:36
  89.2 3.2 %collective-permute-start.26 = (f32[16,256]{1,0:T(8,128)S(1)}, f32[16,256]{1,0:T(8,128)S(1)}, u32[]{:S(2)}, u32[]{:S(2)}) collective-permute-start(f32[16,256]{1,0:T(8,128)S(1)} %rows.3), channel_id=1, source_target_pairs={{0,3},{1,2},{2,1},{3,0},{4,7},{5,6},{6,5},{7,4},{8,11},{9,10},{10,... | collective-permute-start | bytes 49160 | tf_op jit(solution)/shard_map/ppermute | solution.py:36
  89.3 3.8 %collective-permute-start.25 = (f32[16,256]{1,0:T(8,128)S(1)}, f32[16,256]{1,0:T(8,128)S(1)}, u32[]{:S(2)}, u32[]{:S(2)}) collective-permute-start(f32[16,256]{1,0:T(8,128)S(1)} %rows.3), channel_id=1, source_target_pairs={{0,2},{1,3},{2,0},{3,1},{4,6},{5,7},{6,4},{7,5},{8,10},{9,11},{10,... | collective-permute-start | bytes 49160 | tf_op jit(solution)/shard_map/ppermute | solution.py:36
  89.4 3.7 %collective-permute-start.24 = (f32[16,256]{1,0:T(8,128)S(1)}, f32[16,256]{1,0:T(8,128)S(1)}, u32[]{:S(2)}, u32[]{:S(2)}) collective-permute-start(f32[16,256]{1,0:T(8,128)S(1)} %rows.3), channel_id=1, source_target_pairs={{0,1},{1,0},{2,3},{3,2},{4,5},{5,4},{6,7},{7,6},{8,9},{9,8},{10,11... | collective-permute-start | bytes 49160 | tf_op jit(solution)/shard_map/ppermute | solution.py:36
  93.1 5.6 %collective-permute-start.29 = (f32[16,256]{1,0:T(8,128)S(1)}, f32[16,256]{1,0:T(8,128)S(1)}, u32[]{:S(2)}, u32[]{:S(2)}) collective-permute-start(f32[16,256]{1,0:T(8,128)S(1)} %multiply_add_fusion), channel_id=1, source_target_pairs={{0,12},{1,13},{2,14},{3,15},{4,8},{5,9},{6,10},{7,11},{8,4},{9,5},... | collective-permute-start | bytes 49160 | tf_op jit(solution)/shard_map/ppermute | solution.py:36
  94.1 5.0 %collective-permute-start.28 = (f32[16,256]{1,0:T(8,128)S(1)}, f32[16,256]{1,0:T(8,128)S(1)}, u32[]{:S(2)}, u32[]{:S(2)}) collective-permute-start(f32[16,256]{1,0:T(8,128)S(1)} %multiply_add_fusion), channel_id=1, source_target_pairs={{0,8},{1,9},{2,10},{3,11},{4,12},{5,13},{6,14},{7,15},{8,0},{9,1},... | collective-permute-start | bytes 49160 | tf_op jit(solution)/shard_map/ppermute | solution.py:36
  96.2 3.7 %collective-permute-start.27 = (f32[16,256]{1,0:T(8,128)S(1)}, f32[16,256]{1,0:T(8,128)S(1)}, u32[]{:S(2)}, u32[]{:S(2)}) collective-permute-start(f32[16,256]{1,0:T(8,128)S(1)} %multiply_add_fusion), channel_id=1, source_target_pairs={{0,4},{1,5},{2,6},{3,7},{4,0},{5,1},{6,2},{7,3},{8,12},{9,13},{10,... | collective-permute-start | bytes 49160 | tf_op jit(solution)/shard_map/ppermute | solution.py:36
  104.7 3.7 %collective-permute-start.30 = (f32[4,256]{1,0:T(4,128)S(1)}, f32[4,256]{1,0:T(4,128)S(1)}, u32[]{:S(2)}, u32[]{:S(2)}) collective-permute-start(f32[4,256]{1,0:T(4,128)S(1)} %cols.5), channel_id=1, source_target_pairs={{0,16},{16,0},{1,17},{17,1},{2,18},{18,2},{3,19},{19,3},{4,20},{20... | collective-permute-start | bytes 12296 | tf_op jit(solution)/shard_map/ppermute | solution.py:36
  (5 other events, 40.8 us)
